TPU v7x, 32 devices: a whole 2x2x4 slice. The times are simulated.
32 devices in a mesh: wide: 8 (over y, x, core), blk: 4 (over z).
Axes of the slice: x: 2, y: 2, z: 4, core: 2. Of those that a mesh axis runs over, the one named last changes fastest.
Arguments:
- visual_features: bfloat16 [32768, 1152], P(('wide', 'blk')), may hold values from -0.1875 to 0.1875
- sentence_features: bfloat16 [1024, 1152], P(('wide', 'blk')), may hold values from -0.1875 to 0.1875
- true_partner_ids: int32 [32768], P(('wide', 'blk')), may hold values from 0 to 1023
- inverse_warmth: float32 [], replicated, may hold values from 90 to 110
- additive_adjust: float32 [], replicated, may hold values from -12 to -9
Outputs:
- grad_images: float32 [32768, 1152], P(('wide', 'blk'))
- grad_texts: float32 [1024, 1152], P(('wide', 'blk'))
Inputs may be any that keep to these rules, and one draw needn't show every extreme that they name: Image i is paired with text true_partner_ids[i]; a text may be paired with several images or none.
All inputs are finite; a program needn't handle non-finite values.
Results may differ from a plain program's by a relative error of at most 0.007.
Values may be sent and summed in bfloat16 or wider, within the bound.
No kernel may reach another device: no remote copies, remote signals or barrier semaphores. Data moves between devices by JAX's collectives and lax.ppermute only.
A program may use at most 64 MiB of HBM per device.

v0:
```python
import jax
import jax.numpy as jnp
from jax import lax
from jax.sharding import PartitionSpec as P


def remaining_factors(
    visual_features, tile_length, true_partner_ids, leading_offset, inverse_warmth, additive_adjust
):
    cosine_grid = lax.dot_general(
        visual_features, tile_length, (((1,), (1,)), ((), ())), preferred_element_type=jnp.float32
    )
    sigmoid_levels = inverse_warmth * cosine_grid + additive_adjust
    columns = leading_offset + lax.iota(jnp.int32, tile_length.shape[0])
    plus_minus_ones = jnp.where(true_partner_ids[:, None] == columns[None, :], 1.0, -1.0).astype(
        jnp.float32
    )
    return (
        -inverse_warmth * plus_minus_ones * jax.nn.sigmoid(-plus_minus_ones * sigmoid_levels)
    ).astype(jnp.bfloat16)


def both_grads(visual_features, tile_length, loss_grid_scaled):
    incoming_grad_part = jnp.dot(loss_grid_scaled, tile_length, preferred_element_type=jnp.float32)
    returned_grad_part = lax.dot_general(
        loss_grid_scaled,
        visual_features,
        (((0,), (0,)), ((), ())),
        preferred_element_type=jnp.float32,
    )
    return (incoming_grad_part, returned_grad_part)


def shards(visual_features, sentence_features, true_partner_ids, inverse_warmth, additive_adjust):
    width = visual_features.shape[1]
    everything = lax.all_gather(sentence_features, ("wide", "blk"), axis=0, tiled=True)
    total = everything.shape[0]
    block = min(total, 1024)
    count = total // block
    blocks = everything.reshape(count, block, width)

    def scan_step(grad_img, running_dot_sums):
        piece, leading_offset = running_dot_sums
        loss_grid_scaled = remaining_factors(
            visual_features,
            piece,
            true_partner_ids,
            leading_offset,
            inverse_warmth,
            additive_adjust,
        )
        incoming_grad_part, returned_grad_part = both_grads(
            visual_features, piece, loss_grid_scaled
        )
        return (grad_img + incoming_grad_part, returned_grad_part)

    firsts = lax.iota(jnp.int32, count) * block
    grad_images, grad_blocks = lax.scan(
        scan_step, jnp.zeros(visual_features.shape, jnp.float32), (blocks, firsts)
    )
    grad_texts = lax.psum_scatter(
        grad_blocks.reshape(total, width), ("wide", "blk"), scatter_dimension=0, tiled=True
    )
    return (grad_images, grad_texts)


def solution(mesh):
    return jax.shard_map(
        shards,
        mesh=mesh,
        in_specs=(P(("wide", "blk"), None), P(("wide", "blk"), None), P(("wide", "blk")), P(), P()),
        out_specs=(P(("wide", "blk"), None), P(("wide", "blk"), None)),
        check_vma=False,
    )
```

profile of v0, /device:TPU:0, one launch (start us, length us, event | category | flops | bytes accessed | tf_op | source)
XLA Modules:
  0.0 195.8 jit_solution(3945152771545359974)
XLA Ops:
  7.2 0.0 copy-start
  7.2 0.0 all-gather.2.cloned.1.call-start
  7.2 0.7 all-gather.2.cloned.1.call-update
  7.9 0.0 reduce-scatter.2.cloned.1.call-start
  9.3 61.3 %all-gather.2.cloned.1.call-done = bf16[1024,1152]{1,0:T(8,128)(2,1)} async-done(((bf16[32,1152]{1,0:T(8,128)(2,1)}), bf16[1024,1152]{1,0:T(8,128)(2,1)}) %all-gather.2.cloned.1.call-update) | async-done | bytes 2359312 | tf_op jit(solution)/shard_map/all_gather | solution.py:36
  70.6 0.0 copy-done
  70.6 5.9 %fusion.1 = bf16[1024,1024]{1,0:T(8,128)(2,1)S(1)} fusion(bf16[1024,1152]{1,0:T(8,128)(2,1)S(1)} %copy-done, bf16[1024,1152]{1,0:T(8,128)(2,1)} %all-gather.2.cloned.1.call-done, f32[]{:T(128)S(6)} %copy.8, f32[]{:T(128)S(6)} %copy.7, s32[1024]{0:T(1024)} %param.7, f32[]{:T(128)S(6)} %neg.12), kind=kOutput, calls=%fused_computation.3 | convolution fusion | flops 2428502016 | bytes 6819852 | tf_op jit(solution)/shard_map/while/body/eval_jaxpr/dot_general | solution.py:10
  76.5 0.0 copy-start.1
  76.5 1.4 copy-done.1
  77.9 4.6 %fusion.8 = f32[1024,1152]{1,0:T(8,128)} fusion(bf16[1024,1024]{1,0:T(8,128)(2,1)S(1)} %fusion.1, bf16[1024,1152]{1,0:T(8,128)(2,1)S(1)} %copy-done), kind=kOutput, calls=%fused_computation.11 | convolution fusion | flops 2415919104 | bytes 9175040 | tf_op jit(solution)/shard_map/while/body/eval_jaxpr/dot_general | solution.py:25
  82.5 0.0 reduce-scatter.2.cloned.1.call-update
  82.5 7.4 %fusion.7 = f32[1024,1152]{1,0:T(8,128)} fusion(bf16[1024,1024]{1,0:T(8,128)(2,1)} %copy-done.1, bf16[1024,1152]{1,0:T(8,128)(2,1)} %all-gather.2.cloned.1.call-done), kind=kOutput, calls=%fused_computation.10 | convolution fusion | flops 2415919104 | bytes 9175040 | tf_op jit(solution)/shard_map/while/body/eval_jaxpr/dot_general | solution.py:24
  89.9 99.1 %reduce-scatter.2.cloned.1.call-done = f32[32,1152]{1,0:T(8,128)} async-done(((f32[1024,1152]{1,0:T(8,128)}), f32[32,1152]{1,0:T(8,128)}) %reduce-scatter.2.cloned.1.call-update) | async-done | bytes 147472 | tf_op jit(solution)/shard_map/reduce_scatter | solution.py:61
Async XLA Ops:
  7.2 63.4 %copy-start = (bf16[1024,1152]{1,0:T(8,128)(2,1)S(1)}, bf16[1024,1152]{1,0:T(8,128)(2,1)}, u32[]{:S(2)}) copy-start(bf16[1024,1152]{1,0:T(8,128)(2,1)} %param.5) | copy-start | bytes 7077892
  7.2 63.4 %all-gather.2.cloned.1.call-start = ((), (), s32[]{:S(2)}) async-start(), calls=%async_computation.1 | async-start | bytes 2433024 | tf_op jit(solution)/shard_map/all_gather | solution.py:36
  7.9 181.0 %reduce-scatter.2.cloned.1.call-start = ((), (), s32[]{:S(2)}) async-start(), calls=%async_computation.2 | async-start | bytes 4866048 | tf_op jit(solution)/shard_map/reduce_scatter | solution.py:61
  76.5 1.4 copy-start.1
Sparse Core Ops, SparseCore 0:
  10.8 59.7 all-gather.1
  82.6 106.2 reduce-scatter.1
where the time goes:
time: 196 us
  waiting for transfers between devices  161 us (82%)
  matrix products  17.9 us (9%)
  between operations  15.4 us (8%)
    reduce_scatter x1, waiting for transfers between devices, shards(): lax.psum_scatter(grad_blocks.reshape(total, width), ('wide', 'blk'), scat...  99.1 us
    all_gather x1, waiting for transfers between devices, shards(): lax.all_gather(sentence_features, ('wide', 'blk'), axis=0, tiled=True)  61.3 us
    dot_general x1, matrix products, both_grads(): jnp.dot(loss_grid_scaled, tile_length, preferred_element_type=jnp.float32)  7.36 us
    dot_general x1, matrix products, remaining_factors(): lax.dot_general(visual_features, tile_length, (((1,), (1,)), ((), ())), p...  5.92 us
    dot_general x1, matrix products, both_grads(): lax.dot_general(loss_grid_scaled, visual_features, (((0,), (0,)), ((), ()...  4.57 us
  transfers between devices with their start and end apart: 2, of which 2 were waited for; matrix products, arithmetic and copies ran while one was open for 4% of the time, Pallas kernels for 0%

commit v1 on v0

--- a/solution.py
+++ b/solution.py
@@ -2,6 +2,18 @@
 import jax.numpy as jnp
 from jax import lax
 from jax.sharding import PartitionSpec as P
+
+
+def collect(x, axis, dim):
+    ways, here, turn = (lax.axis_size(axis), lax.axis_index(axis), x.shape[dim])
+    line, have = (x, 1)
+    while have < ways:
+        line = jnp.concatenate(
+            [line, lax.ppermute(line, axis, [(d, (d - have) % ways) for d in range(ways)])],
+            axis=dim,
+        )
+        have = 2 * have
+    return jnp.roll(line, here * turn, axis=dim)
 
 
 def remaining_factors(
@@ -33,7 +45,7 @@
 
 def shards(visual_features, sentence_features, true_partner_ids, inverse_warmth, additive_adjust):
     width = visual_features.shape[1]
-    everything = lax.all_gather(sentence_features, ("wide", "blk"), axis=0, tiled=True)
+    everything = collect(sentence_features, ("wide", "blk"), 0)
     total = everything.shape[0]
     block = min(total, 1024)
     count = total // block

time: 196 us -> 215 us (1.097)
  local copies, waits for them, and re-layouts: 1.39 us -> 16.8 us
  starting transfers between devices: 0.08 us -> 9.9 us
  waiting for transfers between devices: 161 us -> 152 us
  other arithmetic: 0 us -> 2.85 us
    all_gather x1 -> x0, waiting for transfers between devices: 61.3 us -> none  [shards(): lax.all_gather(sentence_features, ('wide', 'blk'), axis=0, tiled=True)]
    ppermute x0 -> x5, waiting for transfers between devices: none -> 51.7 us  [collect(): lax.ppermute(line, axis, [(d, (d - have) % ways) for d in range(ways)])]
    unnamed x4 -> x24, local copies, waits for them, and re-layouts: 1.39 us -> 14.5 us
    ppermute x0 -> x5, starting transfers between devices: none -> 9.86 us  [collect(): lax.ppermute(line, axis, [(d, (d - have) % ways) for d in range(ways)])]
    concatenate x0 -> x3, other arithmetic: none -> 2.85 us  [collect(): jnp.concatenate([line, lax.ppermute(line, axis, [(d, (d - have) % ways) f...]
    concatenate x0 -> x2, local copies, waits for them, and re-layouts: none -> 2.28 us  [the longest x1 1.17 us: collect(): jnp.concatenate([line, lax.ppermute(line, axis, [(d, (d - have) % ways) f...]
  transfers between devices with their start and end apart: 2 -> 6, of which waited for: 2 -> 6; matrix products, arithmetic and copies ran while one was open for 4% -> 5% of each run, Pallas kernels for 0% -> 0%
where the time goes in v1:
time: 215 us
  waiting for transfers between devices  152 us (71%)
  matrix products  17.9 us (8%)
  local copies, waits for them, and re-layouts  16.8 us (8%)
  between operations  15.4 us (7%)
  starting transfers between devices  9.9 us (5%)
  other arithmetic  2.85 us (1%)
    reduce_scatter x1, waiting for transfers between devices, shards(): lax.psum_scatter(grad_blocks.reshape(total, width), ('wide', 'blk'), scat...  100 us
    ppermute x5, waiting for transfers between devices, collect(): lax.ppermute(line, axis, [(d, (d - have) % ways) for d in range(ways)])  51.7 us
    unnamed x24, local copies, waits for them, and re-layouts  14.5 us
    ppermute x5, starting transfers between devices, collect(): lax.ppermute(line, axis, [(d, (d - have) % ways) for d in range(ways)])  9.86 us
    dot_general x1, matrix products, both_grads(): jnp.dot(loss_grid_scaled, tile_length, preferred_element_type=jnp.float32)  7.42 us
    dot_general x1, matrix products, remaining_factors(): lax.dot_general(visual_features, tile_length, (((1,), (1,)), ((), ())), p...  5.95 us
    dot_general x1, matrix products, both_grads(): lax.dot_general(loss_grid_scaled, visual_features, (((0,), (0,)), ((), ()...  4.51 us
  transfers between devices with their start and end apart: 6, of which 6 were waited for; matrix products, arithmetic and copies ran while one was open for 5% of the time, Pallas kernels for 0%

profile of v1, /device:TPU:0, one launch (start us, length us, event | category | flops | bytes accessed | tf_op | source)
XLA Modules:
  0.0 214.7 jit_solution(7712883847037105522)
XLA Ops:
  7.2 0.0 copy-start
  7.2 0.0 reduce-scatter.2.cloned.1.call-start
  7.2 6.5 %collective-permute-start = (bf16[32,1152]{1,0:T(8,128)(2,1)}, bf16[32,1152]{1,0:T(8,128)(2,1)S(1)}, u32[]{:S(2)}, u32[]{:S(2)}) collective-permute-start(bf16[32,1152]{1,0:T(8,128)(2,1)} %param.6), channel_id=1, source_target_pairs={{0,31},{1,0},{2,1},{3,2},{4,3},{5,4},{6,5},{7,6},{8,7},{9,8},{10,9... | collective-permute-start | bytes 221192 | tf_op jit(solution)/shard_map/ppermute | solution.py:12
  13.7 2.3 %collective-permute-done = bf16[32,1152]{1,0:T(8,128)(2,1)S(1)} collective-permute-done((bf16[32,1152]{1,0:T(8,128)(2,1)}, bf16[32,1152]{1,0:T(8,128)(2,1)S(1)}, u32[]{:S(2)}, u32[]{:S(2)}) %collective-permute-start) | collective-permute-done | bytes 73760 | tf_op jit(solution)/shard_map/ppermute | solution.py:12
  16.0 0.0 copy-start.5
  16.0 0.9 pad_maximum_fusion.2
  16.9 0.2 collective-permute-start.1
  17.1 8.3 %collective-permute-done.1 = bf16[64,1152]{1,0:T(8,128)(2,1)S(1)} collective-permute-done((bf16[64,1152]{1,0:T(8,128)(2,1)S(1)}, bf16[64,1152]{1,0:T(8,128)(2,1)S(1)}, u32[]{:S(2)}, u32[]{:S(2)}) %collective-permute-start.1) | collective-permute-done | bytes 147488 | tf_op jit(solution)/shard_map/ppermute | solution.py:12
  25.4 0.0 copy-start.3
  25.4 1.0 pad_maximum_fusion.1
  26.4 1.7 collective-permute-start.2
  28.0 1.5 constant_dynamic-update-slice_fusion.4
  29.6 2.7 %collective-permute-done.2 = bf16[128,1152]{1,0:T(8,128)(2,1)S(1)} collective-permute-done((bf16[128,1152]{1,0:T(8,128)(2,1)S(1)}, bf16[128,1152]{1,0:T(8,128)(2,1)S(1)}, u32[]{:S(2)}, u32[]{:S(2)}) %collective-permute-start.2) | collective-permute-done | bytes 294944 | tf_op jit(solution)/shard_map/ppermute | solution.py:12
  32.3 0.0 copy-start.1
  32.3 1.0 pad_maximum_fusion
  33.3 1.2 collective-permute-start.3
  34.4 0.7 constant_dynamic-update-slice_fusion.3
  35.1 0.7 constant_dynamic-update-slice_fusion.2
  35.8 0.8 constant_dynamic-update-slice_fusion.1
  36.7 12.4 %collective-permute-done.3 = bf16[256,1152]{1,0:T(8,128)(2,1)S(1)} collective-permute-done((bf16[256,1152]{1,0:T(8,128)(2,1)S(1)}, bf16[256,1152]{1,0:T(8,128)(2,1)S(1)}, u32[]{:S(2)}, u32[]{:S(2)}) %collective-permute-start.3) | collective-permute-done | bytes 589856 | tf_op jit(solution)/shard_map/ppermute | solution.py:12
  49.0 0.0 copy-start.2
  49.0 0.0 copy-start.6
  49.0 1.2 constant_dynamic-update-slice_fusion
  50.2 0.0 copy-done.1
  50.2 0.0 copy-done.2
  50.2 0.4 collective-permute-start.4
  50.7 0.0 copy-done.5
  50.7 0.0 copy-done.3
  52.0 26.0 %collective-permute-done.4 = bf16[512,1152]{1,0:T(8,128)(2,1)S(1)} collective-permute-done((bf16[512,1152]{1,0:T(8,128)(2,1)}, bf16[512,1152]{1,0:T(8,128)(2,1)S(1)}, u32[]{:S(2)}, u32[]{:S(2)}) %collective-permute-start.4) | collective-permute-done | bytes 1179680 | tf_op jit(solution)/shard_map/ppermute | solution.py:12
  78.0 1.1 constant_dynamic-update-slice_fusion.11
  79.1 1.5 constant_dynamic-update-slice_fusion.10
  80.6 1.5 constant_dynamic-update-slice_fusion.9
  82.1 1.6 constant_dynamic-update-slice_fusion.8
  83.7 1.7 constant_dynamic-update-slice_fusion.7
  85.4 1.9 constant_dynamic-update-slice_fusion.6
  87.3 1.1 constant_dynamic-update-slice_fusion.5
  88.4 0.0 copy-done
  88.4 0.0 copy-done.6
  88.5 5.9 %fusion.1 = bf16[1024,1024]{0,1:T(8,128)(2,1)S(1)} fusion(bf16[1024,1152]{1,0:T(8,128)(2,1)S(1)} %copy-done, f32[]{:T(128)S(6)} %copy.23, f32[]{:T(128)S(6)} %copy.22, s32[1024]{0:T(1024)S(1)} %copy-done.6, f32[]{:T(128)S(6)} %neg.12, bf16[2048,1152]{1,0:T(8,128)(2,1)} %constant_dynamic-update-slice_fusion.5, s32[]{:T(128)S(6)} %select_n.20), kind=kOutput, calls=%fused_computation.3 | convolution fusion | flops 2428502016 | bytes 6819856 | tf_op jit(solution)/shard_map/while/body/eval_jaxpr/dot_general | solution.py:22
  94.4 0.0 copy-start.4
  94.4 1.3 copy-done.4
  95.7 4.5 %fusion.12 = f32[1024,1152]{1,0:T(8,128)} fusion(bf16[1024,1024]{0,1:T(8,128)(2,1)S(1)} %fusion.1, bf16[1024,1152]{1,0:T(8,128)(2,1)S(1)} %copy-done), kind=kOutput, calls=%fused_computation.35 | convolution fusion | flops 2415919104 | bytes 9175040 | tf_op jit(solution)/shard_map/while/body/eval_jaxpr/dot_general | solution.py:37
  100.2 0.0 reduce-scatter.2.cloned.1.call-update
  100.3 7.4 %fusion.7 = f32[1024,1152]{1,0:T(8,128)} fusion(bf16[1024,1024]{0,1:T(8,128)(2,1)} %copy-done.4, bf16[2048,1152]{1,0:T(8,128)(2,1)} %constant_dynamic-update-slice_fusion.5, s32[]{:T(128)S(6)} %select_n.20), kind=kOutput, calls=%fused_computation.10 | convolution fusion | flops 2415919104 | bytes 9175044 | tf_op jit(solution)/shard_map/while/body/eval_jaxpr/dot_general | solution.py:36
  107.7 100.2 %reduce-scatter.2.cloned.1.call-done = f32[32,1152]{1,0:T(8,128)} async-done(((f32[1024,1152]{1,0:T(8,128)}), f32[32,1152]{1,0:T(8,128)}) %reduce-scatter.2.cloned.1.call-update) | async-done | bytes 147472 | tf_op jit(solution)/shard_map/reduce_scatter | solution.py:73
Async XLA Ops:
  7.2 81.3 %copy-start = (bf16[1024,1152]{1,0:T(8,128)(2,1)S(1)}, bf16[1024,1152]{1,0:T(8,128)(2,1)}, u32[]{:S(2)}) copy-start(bf16[1024,1152]{1,0:T(8,128)(2,1)} %param.5) | copy-start | bytes 7077892
  7.2 200.7 %reduce-scatter.2.cloned.1.call-start = ((), (), s32[]{:S(2)}) async-start(), calls=%async_computation.1 | async-start | bytes 4866048 | tf_op jit(solution)/shard_map/reduce_scatter | solution.py:73
  7.2 8.8 %collective-permute-start = (bf16[32,1152]{1,0:T(8,128)(2,1)}, bf16[32,1152]{1,0:T(8,128)(2,1)S(1)}, u32[]{:S(2)}, u32[]{:S(2)}) collective-permute-start(bf16[32,1152]{1,0:T(8,128)(2,1)} %param.6), channel_id=1, source_target_pairs={{0,31},{1,0},{2,1},{3,2},{4,3},{5,4},{6,5},{7,6},{8,7},{9,8},{10,9... | collective-permute-start | bytes 221192 | tf_op jit(solution)/shard_map/ppermute | solution.py:12
  16.0 34.7 %copy-start.5 = (bf16[32,1152]{1,0:T(8,128)(2,1)}, bf16[32,1152]{1,0:T(8,128)(2,1)S(1)}, u32[]{:S(2)}) copy-start(bf16[32,1152]{1,0:T(8,128)(2,1)S(1)} %collective-permute-done) | copy-start | bytes 221188
  16.9 8.5 %collective-permute-start.1 = (bf16[64,1152]{1,0:T(8,128)(2,1)S(1)}, bf16[64,1152]{1,0:T(8,128)(2,1)S(1)}, u32[]{:S(2)}, u32[]{:S(2)}) collective-permute-start(bf16[64,1152]{1,0:T(8,128)(2,1)S(1)} %pad_maximum_fusion.2), channel_id=1, source_target_pairs={{0,30},{1,31},{2,0},{3,1},{4,2},{5,3},{6,4},{7,5},{8,6},{9,7},{10,... | collective-permute-start | bytes 442376 | tf_op jit(solution)/shard_map/ppermute | solution.py:12
  25.4 25.3 %copy-start.3 = (bf16[64,1152]{1,0:T(8,128)(2,1)}, bf16[64,1152]{1,0:T(8,128)(2,1)S(1)}, u32[]{:S(2)}) copy-start(bf16[64,1152]{1,0:T(8,128)(2,1)S(1)} %collective-permute-done.1) | copy-start | bytes 442372
  26.4 5.9 %collective-permute-start.2 = (bf16[128,1152]{1,0:T(8,128)(2,1)S(1)}, bf16[128,1152]{1,0:T(8,128)(2,1)S(1)}, u32[]{:S(2)}, u32[]{:S(2)}) collective-permute-start(bf16[128,1152]{1,0:T(8,128)(2,1)S(1)} %pad_maximum_fusion.1), channel_id=1, source_target_pairs={{0,28},{1,29},{2,30},{3,31},{4,0},{5,1},{6,2},{7,3},{8,4},{9,5},{1... | collective-permute-start | bytes 884744 | tf_op jit(solution)/shard_map/ppermute | solution.py:12
  32.3 17.9 %copy-start.1 = (bf16[128,1152]{1,0:T(8,128)(2,1)}, bf16[128,1152]{1,0:T(8,128)(2,1)S(1)}, u32[]{:S(2)}) copy-start(bf16[128,1152]{1,0:T(8,128)(2,1)S(1)} %collective-permute-done.2) | copy-start | bytes 884740
  33.3 15.8 %collective-permute-start.3 = (bf16[256,1152]{1,0:T(8,128)(2,1)S(1)}, bf16[256,1152]{1,0:T(8,128)(2,1)S(1)}, u32[]{:S(2)}, u32[]{:S(2)}) collective-permute-start(bf16[256,1152]{1,0:T(8,128)(2,1)S(1)} %pad_maximum_fusion), channel_id=1, source_target_pairs={{0,24},{1,25},{2,26},{3,27},{4,28},{5,29},{6,30},{7,31},{8,0},{9,1... | collective-permute-start | bytes 1769480 | tf_op jit(solution)/shard_map/ppermute | solution.py:12
  49.0 1.2 copy-start.2
  49.0 39.4 %copy-start.6 = (s32[1024]{0:T(1024)S(1)}, s32[1024]{0:T(1024)}, u32[]{:S(2)}) copy-start(s32[1024]{0:T(1024)} %param.7) | copy-start | bytes 12292
  50.2 27.7 %collective-permute-start.4 = (bf16[512,1152]{1,0:T(8,128)(2,1)}, bf16[512,1152]{1,0:T(8,128)(2,1)S(1)}, u32[]{:S(2)}, u32[]{:S(2)}) collective-permute-start(bf16[512,1152]{1,0:T(8,128)(2,1)} %get-tuple-element.18), channel_id=1, source_target_pairs={{0,16},{1,17},{2,18},{3,19},{4,20},{5,21},{6,22},{7,23},{8,24},{9,... | collective-permute-start | bytes 3538952 | tf_op jit(solution)/shard_map/ppermute | solution.py:12
  94.4 1.3 copy-start.4
Sparse Core Ops, SparseCore 0:
  100.4 107.4 reduce-scatter.1
